TPU v7x, 32 devices: a whole 2x2x4 slice. The times are simulated.
32 devices in a mesh: band: 8 (over z, x), lon: 4 (over y, core).
Axes of the slice: x: 2, y: 2, z: 4, core: 2. Of those that a mesh axis runs over, the one named last changes fastest.
Arguments:
- coefficients: bfloat16 [8, 640, 4, 64], P('lon', 'band'), may hold values from -6 to 6
- cycle_length: int32 [64], replicated, may hold values from 20 to 5136, as said below
- row_latitude: int32 [64], replicated, may hold values from 0 to 63, each once
- pair_band: int32 [640], replicated, may hold values from 0 to 7, as said below
- gridpoint_factor: bfloat16 [64, 5632], P('band', 'lon'), may hold values from 0.5 to 2
Outputs:
- grid_values: bfloat16 [8, 64, 5632], P(None, 'band', 'lon')
- tendencies: bfloat16 [8, 640, 4, 64], P('lon', 'band')
Inputs may be any that keep to these rules, and one draw needn't show every extreme that they name: `cycle_length`: each entry is 20 + 4 i for a whole number i; some entry equals 5136. `pair_band`: each band owns at most 80 pairs and some band owns exactly that many. `row_latitude`: each latitude appears once.
All inputs are finite; a program needn't handle non-finite values.
Results may differ from a plain program's by a relative error of at most 0.0068.
Values may be sent and summed in bfloat16 or wider, within the bound.
A program may use at most 128 MiB of HBM per device.

v0:
```python
import functools
import math

import jax
import jax.numpy as jnp
import numpy as np
from jax import lax
from jax.experimental import pallas as pl
from jax.experimental.pallas import tpu as pltpu
from jax.sharding import PartitionSpec as P

TWO_PI = 2.0 * math.pi
LANES = 128
CHUNK = 256


def cos_sin(product, length, inverse):
    turns = jnp.floor(product * inverse + 0.5)
    half = (product - turns * length) * (inverse * (0.5 * TWO_PI))
    square = half * half
    sine = jnp.full_like(half, -1.0 / math.factorial(11))
    for order in (9, 7, 5, 3, 1):
        sine = sine * square + (-1.0) ** (order // 2) / math.factorial(order)
    sine = sine * half
    cosine = jnp.full_like(half, 1.0 / math.factorial(12))
    for order in (10, 8, 6, 4, 2, 0):
        cosine = cosine * square + (-1.0) ** (order // 2) / math.factorial(order)
    return 1.0 - 2.0 * sine * sine, 2.0 * sine * cosine


MESH = pl.DeviceIdType.MESH


def round_kernel(
    bands,
    lanes,
    cycle_ref,
    latitude_ref,
    order_ref,
    pair_band_ref,
    leaving,
    factor_ref,
    blocks,
    returned,
    arrived,
    cycles,
    grid_ref,
    result,
    hot,
    ordered,
    finished,
    lhs,
    total,
    row_factor,
    cos_state,
    sin_state,
    cos_step,
    sin_step,
    cos_high,
    sin_high,
    cos_high_step,
    sin_high_step,
    send_sem,
    recv_sem,
    back_send_sem,
    back_recv_sem,
    factor_send_sem,
    factor_recv_sem,
    grid_send_sem,
    grid_recv_sem,
):
    band, lane = lax.axis_index("band"), lax.axis_index("lon")
    me = band * lanes + lane
    devices = bands * lanes
    band_rows, points = factor_ref.shape
    rows, fields = grid_ref.shape[0], grid_ref.shape[1]
    slots, waves = hot.shape
    high = waves // LANES
    half = waves // 2
    stacked = leaving.shape[1] * lanes

    def peer(k):
        flat = lax.rem(me + k, devices)
        return flat, {"band": flat // lanes, "lon": lax.rem(flat, lanes)}

    def block_of(index):
        return pl.ds(pl.multiple_of(index * points, LANES), points)

    def send_chunks(source, target, sent, received):
        def send(k, carry):
            flat, device = peer(k)
            pltpu.make_async_remote_copy(
                src_ref=source.at[flat],
                dst_ref=target.at[me],
                send_sem=sent,
                recv_sem=received,
                device_id=device,
                device_id_type=MESH,
            ).start()
            return carry

        lax.fori_loop(1, devices, send, 0)
        target[me] = source[me]

    def wait_chunks(source, target, sent, received):
        pltpu.make_async_remote_copy(
            src_ref=source.at[pl.ds(0, devices - 1)],
            dst_ref=target.at[pl.ds(0, devices - 1)],
            send_sem=sent,
            recv_sem=received,
            device_id={"band": band, "lon": lane},
            device_id_type=MESH,
        ).wait()

    def factor_copy(j):
        return pltpu.make_async_remote_copy(
            src_ref=factor_ref,
            dst_ref=cycles.at[:, block_of(lane)],
            send_sem=factor_send_sem.at[j],
            recv_sem=factor_recv_sem.at[j],
            device_id={"lon": lax.rem(lane + j, lanes)},
            device_id_type=MESH,
        )

    def grid_copy(i, j):
        other = lax.rem(lane + j, lanes)
        return pltpu.make_async_remote_copy(
            src_ref=grid_ref.at[i, :, block_of(other)],
            dst_ref=blocks.at[lane, i],
            send_sem=grid_send_sem.at[i, j],
            recv_sem=grid_recv_sem.at[i, j],
            device_id={"lon": other},
            device_id_type=MESH,
        )

    barrier = pltpu.get_barrier_semaphore()

    def signal(k, carry):
        pl.semaphore_signal(barrier, inc=1, device_id=peer(k)[1], device_id_type=MESH)
        return carry

    lax.fori_loop(1, devices, signal, 0)

    pair_band = pair_band_ref[...].reshape(1, half)
    source = lax.broadcasted_iota(jnp.int32, (half, half), 0)
    target = lax.broadcasted_iota(jnp.int32, (half, half), 1)
    earlier = jnp.where(source < target, 1.0, 0.0).astype(jnp.bfloat16)
    mirror = jnp.where(source == half - 1 - target, 1.0, 0.0).astype(jnp.bfloat16)
    padded_bands = -(-bands // 8) * 8
    owner = lax.broadcasted_iota(jnp.int32, (padded_bands, half), 0) == pair_band
    counts = jnp.dot(
        jnp.where(owner, 1.0, 0.0).astype(jnp.bfloat16), earlier, preferred_element_type=jnp.float32
    )
    place = jnp.sum(jnp.where(owner, counts, 0.0), axis=0, keepdims=True)
    pair = jnp.concatenate([pair_band.astype(jnp.float32)] * 4 + [place] * 4, axis=0)
    flipped = jnp.dot(pair.astype(jnp.bfloat16), mirror, preferred_element_type=jnp.float32)
    both = jnp.concatenate([pair, flipped], axis=1)
    slot_of_wave = (both[0:1] * LANES + both[4:5]).astype(jnp.int32)

    def fill(step, carry):
        start = pl.multiple_of(step * 32, 32)
        slot = lax.broadcasted_iota(jnp.int32, (32, waves), 0) + start
        hot[pl.ds(start, 32), :] = jnp.where(slot == slot_of_wave, 1.0, 0.0).astype(jnp.bfloat16)
        return carry

    lax.fori_loop(0, slots // 32, fill, 0)

    pl.semaphore_wait(barrier, devices - 1)
    send_chunks(leaving, arrived, send_sem, recv_sem)
    for j in range(1, lanes):
        factor_copy(j).start()
    cycles[:, block_of(lane)] = factor_ref[...]

    wave = lax.broadcasted_iota(jnp.int32, (1, waves), 1)

    def length_of(i):
        row = jnp.minimum(lane * rows + i, band_rows - 1)
        n = cycle_ref[latitude_ref[band * band_rows + row]]
        length = jnp.full((1, 1), n, jnp.int32).astype(jnp.float32)
        return row, n, length, 1.0 / length

    def prepare(i, carry):
        row, n, length, inverse = length_of(i)
        low_wave = lax.broadcasted_iota(jnp.int32, (LANES, CHUNK), 0).astype(jnp.float32)
        place = lax.broadcasted_iota(jnp.int32, (LANES, CHUNK), 1).astype(jnp.float32)
        cos_state[i], sin_state[i] = cos_sin(low_wave * place, length, inverse)
        step_wave = lax.broadcasted_iota(jnp.int32, (LANES, LANES), 0).astype(jnp.float32)
        cos_step[i], sin_step[i] = cos_sin(step_wave * float(CHUNK), length, inverse)
        padded = cos_high.shape[1]
        high_wave = LANES * lax.broadcasted_iota(jnp.int32, (padded, CHUNK), 0)
        high_place = lax.broadcasted_iota(jnp.int32, (padded, CHUNK), 1)
        cos_high[i], sin_high[i] = cos_sin(
            (high_wave * high_place).astype(jnp.float32), length, inverse
        )
        cos_high_step[i], sin_high_step[i] = cos_sin(
            (high_wave * CHUNK).astype(jnp.float32), length, inverse
        )
        return carry

    lax.fori_loop(0, rows, prepare, 0)

    wait_chunks(leaving, arrived, send_sem, recv_sem)

    pieces = []
    for b in range(bands):
        piece = arrived[b * lanes : (b + 1) * lanes].astype(jnp.float32)
        pieces.append(piece.reshape(stacked, LANES).astype(jnp.bfloat16))
    by_part = jnp.dot(
        order_ref[...], jnp.concatenate(pieces, axis=1), preferred_element_type=jnp.float32
    ).astype(jnp.bfloat16)
    for member in range(2):
        columns = slice(member * half, (member + 1) * half)
        ordered[:, columns] = jnp.dot(
            by_part[member * stacked // 2 : (member + 1) * stacked // 2],
            hot[:, columns],
            preferred_element_type=jnp.float32,
        )

    for j in range(1, lanes):
        factor_copy(j).wait()

    def one_row(i, carry):
        row, n, length, inverse = length_of(i)
        norm = lax.rsqrt(length)
        kept = jnp.where(2 * wave < n, 1.0, 0.0)
        weight = kept * jnp.where(wave == 0, 1.0, 2.0)
        chosen = lax.broadcasted_iota(jnp.int32, (band_rows, 1), 0) == row
        row_factor[...] = jnp.sum(
            jnp.where(chosen, cycles[...].astype(jnp.float32), 0.0), axis=0, keepdims=True
        )
        for t in range(2):
            own = pl.ds(pl.multiple_of((t * rows + i) * fields, fields), fields)
            weighted = (ordered[own, :] * weight).astype(jnp.bfloat16)
            for b in range(high):
                part = weighted[:, b * LANES : (b + 1) * LANES]
                if t == 0:
                    lhs[b * fields : (b + 1) * fields, 0:LANES] = part
                    lhs[(high + b) * fields : (high + b + 1) * fields, LANES : 2 * LANES] = -part
                else:
                    lhs[b * fields : (b + 1) * fields, LANES : 2 * LANES] = part
                    lhs[(high + b) * fields : (high + b + 1) * fields, 0:LANES] = part

        total[...] = jnp.zeros_like(total)

        def chunk(h, carry):
            columns = pl.ds(pl.multiple_of(h * CHUNK, CHUNK), CHUNK)
            cosine, sine = cos_state[i], sin_state[i]
            table = jnp.concatenate([cosine, -sine], axis=0).astype(jnp.bfloat16)
            found = jnp.dot(lhs[...], table, preferred_element_type=jnp.float32)
            high_cos, high_sin = cos_high[i], sin_high[i]
            value = jnp.zeros((fields, CHUNK), jnp.float32)
            for b in range(high):
                real = found[b * fields : (b + 1) * fields]
                imag = found[(high + b) * fields : (high + b + 1) * fields]
                value = value + (real * high_cos[b : b + 1] - imag * high_sin[b : b + 1])
            at = h * CHUNK + lax.broadcasted_iota(jnp.int32, (1, CHUNK), 1)
            value = jnp.where(at < n, value * norm, 0.0).astype(jnp.bfloat16)
            grid_ref[i, :, columns] = value
            product = row_factor[:, columns] * value.astype(jnp.float32)
            product = product.astype(jnp.bfloat16).astype(jnp.float32)
            turned = [product * high_cos[b : b + 1] for b in range(high)]
            turned += [product * (-high_sin[b : b + 1]) for b in range(high)]
            turned = jnp.concatenate(turned, axis=0).astype(jnp.bfloat16)
            total[...] += lax.dot_general(
                turned, table, (((1,), (1,)), ((), ())), preferred_element_type=jnp.float32
            )
            step_cos = jnp.concatenate([cos_step[i]] * (CHUNK // LANES), axis=1)
            step_sin = jnp.concatenate([sin_step[i]] * (CHUNK // LANES), axis=1)
            cos_state[i] = cosine * step_cos - sine * step_sin
            sin_state[i] = sine * step_cos + cosine * step_sin
            high_step_cos, high_step_sin = cos_high_step[i], sin_high_step[i]
            cos_high[i] = high_cos * high_step_cos - high_sin * high_step_sin
            sin_high[i] = high_sin * high_step_cos + high_cos * high_step_sin
            return carry

        lax.fori_loop(0, lanes * points // CHUNK, chunk, 0, unroll=True)

        for j in range(1, lanes):
            grid_copy(i, j).start()
        blocks[lane, i] = grid_ref[i, :, block_of(lane)]

        scale = kept * norm
        for t in range(2):
            pieces = []
            for b in range(high):
                real = slice(b * fields, (b + 1) * fields)
                imag = slice((high + b) * fields, (high + b + 1) * fields)
                if t == 0:
                    pieces.append(total[real, 0:LANES] - total[imag, LANES : 2 * LANES])
                else:
                    pieces.append(total[imag, 0:LANES] + total[real, LANES : 2 * LANES])
            own = pl.ds(pl.multiple_of((t * rows + i) * fields, fields), fields)
            finished[own, :] = jnp.concatenate(pieces, axis=1) * scale
        return carry

    lax.fori_loop(0, rows, one_row, 0, unroll=True)
    pieces = []
    for member in range(2):
        columns = slice(member * half, (member + 1) * half)
        pieces.append(
            lax.dot_general(
                finished[:, columns].astype(jnp.bfloat16),
                hot[:, columns],
                (((1,), (1,)), ((), ())),
                preferred_element_type=jnp.float32,
            )
        )
    by_part = jnp.concatenate(pieces, axis=0).astype(jnp.bfloat16)
    by_lane = lax.dot_general(
        order_ref[...], by_part, (((0,), (0,)), ((), ())), preferred_element_type=jnp.float32
    )
    for b in range(bands):
        piece = by_lane[:, b * LANES : (b + 1) * LANES].reshape(lanes, stacked // lanes, LANES)
        result[b * lanes : (b + 1) * lanes] = piece.astype(jnp.bfloat16)

    send_chunks(result, returned, back_send_sem, back_recv_sem)
    for i in range(rows):
        for j in range(1, lanes):
            grid_copy(i, j).wait()
    wait_chunks(result, returned, back_send_sem, back_recv_sem)


def round_trip(cycle_length, held, order, pair_band, leaving, factor, bands, lanes, fields):
    devices, chunk_rows, _ = leaving.shape
    band_rows, points = factor.shape
    waves = 2 * pair_band.shape[0]
    rows = -(-band_rows // lanes)
    high = waves // LANES
    padded = -(-high // 8) * 8
    stacked = 2 * high * fields
    chunks = (devices, chunk_rows, LANES)
    return pl.pallas_call(
        functools.partial(round_kernel, bands, lanes),
        in_specs=[pl.BlockSpec(memory_space=pltpu.SMEM)] * 2
        + [pl.BlockSpec(memory_space=pltpu.VMEM)] * 4,
        out_specs=[pl.BlockSpec(memory_space=pltpu.VMEM)] * 2,
        scratch_shapes=[
            pltpu.VMEM(chunks, jnp.bfloat16),
            pltpu.VMEM((band_rows, lanes * points), jnp.bfloat16),
            pltpu.VMEM((rows, fields, lanes * points), jnp.bfloat16),
            pltpu.VMEM(chunks, jnp.bfloat16),
            pltpu.VMEM((bands * LANES, waves), jnp.bfloat16),
            pltpu.VMEM((2 * rows * fields, waves), jnp.float32),
            pltpu.VMEM((2 * rows * fields, waves), jnp.float32),
            pltpu.VMEM((stacked, 2 * LANES), jnp.bfloat16),
            pltpu.VMEM((stacked, 2 * LANES), jnp.float32),
            pltpu.VMEM((1, lanes * points), jnp.float32),
            pltpu.VMEM((rows, LANES, CHUNK), jnp.float32),
            pltpu.VMEM((rows, LANES, CHUNK), jnp.float32),
            pltpu.VMEM((rows, LANES, LANES), jnp.float32),
            pltpu.VMEM((rows, LANES, LANES), jnp.float32),
            pltpu.VMEM((rows, padded, CHUNK), jnp.float32),
            pltpu.VMEM((rows, padded, CHUNK), jnp.float32),
            pltpu.VMEM((rows, padded, CHUNK), jnp.float32),
            pltpu.VMEM((rows, padded, CHUNK), jnp.float32),
        ]
        + [pltpu.SemaphoreType.DMA] * 4
        + [pltpu.SemaphoreType.DMA((lanes,))] * 2
        + [pltpu.SemaphoreType.DMA((rows, lanes))] * 2,
        out_shape=[
            jax.ShapeDtypeStruct((lanes, rows, fields, points), jnp.bfloat16),
            jax.ShapeDtypeStruct(chunks, jnp.bfloat16),
        ],
        compiler_params=pltpu.CompilerParams(
            collective_id=0,
            has_side_effects=True,
            vmem_limit_bytes=(12 << 20) + 4 * bands * LANES * waves,
        ),
    )(cycle_length, held, order, pair_band, leaving, factor)


def on_device(coefficients, cycle_length, row_latitude, pair_band, gridpoint_factor):
    bands, lanes = lax.axis_size("band"), lax.axis_size("lon")
    devices = bands * lanes
    own_fields, slot_count, parts, latitudes = coefficients.shape
    band_rows, points = gridpoint_factor.shape
    fields = own_fields * lanes
    own_rows = -(-band_rows // lanes)
    lane_rows = np.arange(lanes * own_rows)
    inside = np.tile(lane_rows < band_rows, bands)
    clamped = np.minimum(lane_rows, band_rows - 1)
    row_ids = (np.arange(bands)[:, None] * band_rows + clamped[None, :]).reshape(-1)
    held = row_latitude if inside.all() else jnp.take(row_latitude, row_ids)
    onehot = held[:, None] == jnp.arange(latitudes, dtype=jnp.int32)[None, :]
    leaving = jnp.einsum(
        "rl,fstl->rtfs",
        onehot.astype(jnp.bfloat16),
        coefficients,
        preferred_element_type=jnp.float32,
    ).astype(jnp.bfloat16)
    leaving = jnp.pad(leaving, ((0, 0), (0, 0), (0, 0), (0, LANES - slot_count)))
    chunk_rows = own_rows * parts * own_fields
    leaving = leaving.reshape(devices, chunk_rows, LANES)
    places = np.arange(lanes * chunk_rows).reshape(lanes, own_rows, parts, own_fields)
    places = places.transpose(2, 1, 0, 3).reshape(-1)
    order = jnp.asarray(
        places[:, None] == np.arange(lanes * chunk_rows)[None, :], dtype=jnp.bfloat16
    )
    blocks, returned = round_trip(
        cycle_length,
        row_latitude,
        order,
        pair_band,
        leaving,
        gridpoint_factor,
        bands,
        lanes,
        fields,
    )
    grid_rows = blocks.reshape(lanes * own_rows, fields, points)[:band_rows]
    grid_rows = jnp.transpose(grid_rows, (1, 0, 2))
    returned = returned.reshape(devices * own_rows, parts, own_fields, LANES)
    back = onehot & inside[:, None]
    tendencies = jnp.einsum(
        "rtfs,rl->fstl",
        returned[..., :slot_count],
        back.astype(jnp.bfloat16),
        preferred_element_type=jnp.float32,
    ).astype(jnp.bfloat16)
    return (grid_rows, tendencies)


def solution(mesh):
    return jax.shard_map(
        on_device,
        mesh=mesh,
        in_specs=(P("lon", "band", None, None), P(), P(), P(), P("band", "lon")),
        out_specs=(P(None, "band", "lon"), P("lon", "band", None, None)),
        check_vma=False,
    )
```

profile of v0, /device:TPU:0, one launch (start us, length us, event | category | flops | bytes accessed | tf_op | source)
XLA Modules:
  0.0 29.7 jit_solution(4722564872617865267)
XLA Ops:
  0.6 0.0 copy-start
  0.6 0.9 %copy-done = bf16[2,80,4,64]{1,3,2,0:T(8,128)(2,1)S(1)} copy-done((bf16[2,80,4,64]{1,3,2,0:T(8,128)(2,1)S(1)}, bf16[2,80,4,64]{1,3,2,0:T(8,128)(2,1)}, u32[]{:S(2)}) %copy-start) | copy-done | bytes 81944
  1.5 0.9 %fusion = bf16[64,4,2,80]{3,0,1,2:T(8,128)(2,1)S(1)} fusion(bf16[2,80,4,64]{1,3,2,0:T(8,128)(2,1)S(1)} %copy-done, s32[64]{0:T(128)} %latitude_ref.1), kind=kOutput, calls=%fused_computation.2 | convolution fusion | flops 5287936 | bytes 164096 | tf_op jit(solution)/shard_map/rl,fstl->rtfs/dot_general | solution.py:385
  2.4 0.1 copy.18
  2.6 0.0 copy-start.1
  2.6 0.0 copy-start.2
  2.6 0.0 copy-start.4
  2.6 0.1 pad.4.clone
  2.8 0.0 copy-start.3
  2.8 0.0 copy-start.5
  2.8 0.5 %copy-done.1 = bf16[8,1408]{1,0:T(8,128)(2,1)S(1)} copy-done((bf16[8,1408]{1,0:T(8,128)(2,1)S(1)}, bf16[8,1408]{1,0:T(8,128)(2,1)}, u32[]{:S(2)}) %copy-start.1) | copy-done | bytes 22552
  3.3 0.0 copy-done.2
  3.3 0.0 copy-done.4
  3.3 0.1 copy-done.3
  3.4 0.0 copy-done.5
  3.4 24.8 %shard_map.86 = (bf16[4,2,8,1408]{3,2,1,0:T(8,128)(2,1)S(1)}, bf16[32,16,128]{2,1,0:T(8,128)(2,1)S(1)}) custom-call(s32[64]{0:T(128)S(1)} %copy-done.5, s32[64]{0:T(128)S(1)} %copy-done.3, bf16[64,64]{1,0:T(8,128)(2,1)S(1)} %copy-done.2, s32[640]{0:T(1024)S(1)} %copy-done.4, bf16[32,16,128]{2,1,0:T(8,128)(2,1)S(1)} %bitcast.19, bf16[8,1408]{1,0:T(8,128)(2,1)S(1)} %copy-done.1), custom_call_target="tpu_custom_call" | custom-call | tf_op jit(solution)/shard_map/pallas_call | solution.py:332
  28.2 0.7 %copy.22 = bf16[8,8,1408]{2,0,1:T(8,128)(2,1)} copy(bf16[8,8,1408]{2,1,0:T(8,128)(2,1)S(1)} %bitcast.20) | data formatting | bytes 360448 | tf_op jit(solution)/shard_map/reshape | solution.py:410
  28.9 0.2 fusion.1
  29.1 0.7 %copy.13 = bf16[2,80,4,64]{1,3,2,0:T(8,128)(2,1)} copy(bf16[2,80,4,64]{1,3,0,2:T(8,128)(2,1)S(1)} %fusion.1) | data formatting | bytes 163840
Async XLA Ops:
  0.6 0.9 %copy-start = (bf16[2,80,4,64]{1,3,2,0:T(8,128)(2,1)S(1)}, bf16[2,80,4,64]{1,3,2,0:T(8,128)(2,1)}, u32[]{:S(2)}) copy-start(bf16[2,80,4,64]{1,3,2,0:T(8,128)(2,1)} %param.7) | copy-start | bytes 245764
  2.6 0.7 %copy-start.1 = (bf16[8,1408]{1,0:T(8,128)(2,1)S(1)}, bf16[8,1408]{1,0:T(8,128)(2,1)}, u32[]{:S(2)}) copy-start(bf16[8,1408]{1,0:T(8,128)(2,1)} %factor_ref.1) | copy-start | bytes 67588
  2.6 0.7 %copy-start.2 = (bf16[64,64]{1,0:T(8,128)(2,1)S(1)}, bf16[64,64]{1,0:T(8,128)(2,1)}, u32[]{:S(2)}) copy-start(bf16[64,64]{1,0:T(8,128)(2,1)} %constant.7.clone.order_ref) | copy-start | bytes 24580
  2.6 0.7 %copy-start.4 = (s32[640]{0:T(1024)S(1)}, s32[640]{0:T(1024)}, u32[]{:S(2)}) copy-start(s32[640]{0:T(1024)} %pair_band_ref.1) | copy-start | bytes 7684
  2.8 0.7 %copy-start.3 = (s32[64]{0:T(128)S(1)}, s32[64]{0:T(128)}, u32[]{:S(2)}) copy-start(s32[64]{0:T(128)} %latitude_ref.1) | copy-start | bytes 772
  2.8 0.7 %copy-start.5 = (s32[64]{0:T(128)S(1)}, s32[64]{0:T(128)}, u32[]{:S(2)}) copy-start(s32[64]{0:T(128)} %cycle_ref.1) | copy-start | bytes 772
where the time goes:
time: 29.9 us; the launch traced here: 29.7 us
  Pallas kernels  24.8 us (83%)
  local copies, waits for them, and re-layouts  3.21 us (11%)
  matrix products  1.04 us (3%)
  between operations  0.72 us (2%)
    pallas_call x1, Pallas kernels, round_trip(): pl.pallas_call(functools.partial(round_kernel, bands, lanes), in_specs=[p...  24.8 us
    unnamed x14, local copies, waits for them, and re-layouts  2.38 us
    dot_general x1, matrix products, on_device(): jnp.einsum('rl,fstl->rtfs', onehot.astype(jnp.bfloat16), coefficients, pr...  0.88 us
    reshape x1, local copies, waits for them, and re-layouts, on_device(): grid_rows = blocks.reshape(lanes * own_rows, fields, points)[:band_rows]  0.69 us

commit v1 on v0

v1 whole, which is shorter than its diff:
```python
import functools
import math

import jax
import jax.numpy as jnp
import numpy as np
from jax import lax
from jax.experimental import pallas as pl
from jax.experimental.pallas import tpu as pltpu
from jax.sharding import PartitionSpec as P

TWO_PI = 2.0 * math.pi
LANES = 128
CHUNK = 256
GROUP = 64
MESH = pl.DeviceIdType.MESH


def cos_sin(product, length, inverse):
    turns = jnp.floor(product * inverse + 0.5)
    half = (product - turns * length) * (inverse * (0.5 * TWO_PI))
    square = half * half
    sine = jnp.full_like(half, -1.0 / math.factorial(11))
    for order in (9, 7, 5, 3, 1):
        sine = sine * square + (-1.0) ** (order // 2) / math.factorial(order)
    sine = sine * half
    cosine = jnp.full_like(half, 1.0 / math.factorial(12))
    for order in (10, 8, 6, 4, 2, 0):
        cosine = cosine * square + (-1.0) ** (order // 2) / math.factorial(order)
    return 1.0 - 2.0 * sine * sine, 2.0 * sine * cosine


def round_kernel(
    bands,
    lanes,
    coefficients_hbm,
    cycle_hbm,
    latitude_hbm,
    pair_band_hbm,
    factor_hbm,
    order_hbm,
    blocks,
    tendencies,
    coefficients,
    cycle_ref,
    latitude_ref,
    pair_band_ref,
    factor_ref,
    order_ref,
    pick,
    leaving,
    arrived,
    result,
    returned,
    cycles,
    grid_ref,
    table,
    lhs,
    product_ref,
    row_factor,
    wave_column,
    step_ref,
    weight_ref,
    finished,
    input_sem,
    send_sem,
    recv_sem,
    back_send_sem,
    back_recv_sem,
    factor_send_sem,
    factor_recv_sem,
    grid_send_sem,
    grid_recv_sem,
):
    band, lane = lax.axis_index("band"), lax.axis_index("lon")
    me = band * lanes + lane
    devices = bands * lanes
    band_rows, points = factor_ref.shape
    rows, fields = grid_ref.shape[0], grid_ref.shape[1]
    own_fields, parts, latitudes, slot_count = coefficients.shape
    half = pair_band_ref.shape[-1]
    waves = 2 * half
    padded = wave_column.shape[0]
    width = 2 * padded
    cycle_points = lanes * points
    chunks = cycle_points // CHUNK
    entry = parts * own_fields
    entries = devices * rows
    chunk_rows = rows * entry
    stacked = chunk_rows * lanes
    groups = entries // GROUP
    group_devices = GROUP // rows
    unroll = devices <= 32

    def peer(k):
        flat = lax.rem(me + k, devices)
        return flat, {"band": flat // lanes, "lon": lax.rem(flat, lanes)}

    def block_of(index):
        return pl.ds(pl.multiple_of(index * points, LANES), points)

    def send_chunks(source, target, sent, received, far_first):
        def send(k, carry):
            flat, device = peer(devices - k if far_first else k)
            pltpu.make_async_remote_copy(
                src_ref=source.at[flat],
                dst_ref=target.at[me],
                send_sem=sent,
                recv_sem=received,
                device_id=device,
                device_id_type=MESH,
            ).start()
            return carry

        lax.fori_loop(1, devices, send, 0, unroll=unroll)
        target[me] = source[me]

    def wait_chunks(source, target, sent, received):
        pltpu.make_async_remote_copy(
            src_ref=source.at[pl.ds(0, devices - 1)],
            dst_ref=target.at[pl.ds(0, devices - 1)],
            send_sem=sent,
            recv_sem=received,
            device_id={"band": band, "lon": lane},
            device_id_type=MESH,
        ).wait()

    def factor_copy(j):
        return pltpu.make_async_remote_copy(
            src_ref=factor_ref,
            dst_ref=cycles.at[:, block_of(lane)],
            send_sem=factor_send_sem.at[j],
            recv_sem=factor_recv_sem.at[j],
            device_id={"lon": lax.rem(lane + j, lanes)},
            device_id_type=MESH,
        )

    def grid_copy(i, j):
        other = lax.rem(lane + j, lanes)
        return pltpu.make_async_remote_copy(
            src_ref=grid_ref.at[i, :, block_of(other)],
            dst_ref=blocks.at[lane, i],
            send_sem=grid_send_sem.at[i, j],
            recv_sem=grid_recv_sem.at[i, j],
            device_id={"lon": other},
            device_id_type=MESH,
        )

    barrier = pltpu.get_barrier_semaphore()

    def signal(k, carry):
        pl.semaphore_signal(barrier, inc=1, device_id=peer(k)[1], device_id_type=MESH)
        return carry

    inputs = [
        pltpu.make_async_copy(source, target, input_sem.at[index])
        for index, (source, target) in enumerate(
            (
                (latitude_hbm, latitude_ref),
                (coefficients_hbm, coefficients),
                (pair_band_hbm, pair_band_ref),
                (cycle_hbm, cycle_ref),
                (factor_hbm, factor_ref),
                (order_hbm, order_ref),
            )
        )
    ]
    lax.fori_loop(1, devices, signal, 0, unroll=unroll)
    for copy in inputs:
        copy.start()

    size = latitudes * entry
    part_row = lax.broadcasted_iota(jnp.int32, (entry, size), 0)
    offset = (lax.rem(part_row, own_fields) * parts + part_row // own_fields) * latitudes
    latitude_of = lax.broadcasted_iota(jnp.int32, (entry, size), 1) - offset

    def fill_pick(group):
        def one(pair, carry):
            pieces = []
            for side in range(2):
                number = group * GROUP + pair * 2 + side
                device, i = number // rows, lax.rem(number, rows)
                local = lax.rem(device, lanes) * rows + i
                row = (device // lanes) * band_rows + jnp.minimum(local, band_rows - 1)
                held = jnp.where(local < band_rows, latitude_ref[row], -(1 << 20))
                pieces.append(jnp.where(latitude_of == held, 1.0, 0.0))
            start = pl.multiple_of(pair * 2 * entry, 2 * entry)
            pick[pl.ds(start, 2 * entry), :] = jnp.concatenate(pieces, axis=0).astype(jnp.bfloat16)
            return carry

        lax.fori_loop(0, GROUP // 2, one, 0, unroll=4)

    def devices_of(group):
        return pl.ds(group * group_devices, group_devices)

    leaving[...] = jnp.zeros_like(leaving)
    inputs[0].wait()

    def gather(group, carry):
        fill_pick(group)
        if groups > 1:
            inputs_ready = coefficients[...]
        else:
            inputs[1].wait()
            inputs_ready = coefficients[...]
        picked = jnp.dot(
            pick[...], inputs_ready.reshape(size, slot_count), preferred_element_type=jnp.float32
        )
        picked = picked.reshape(group_devices, chunk_rows, slot_count).astype(jnp.bfloat16)
        leaving[devices_of(group), :, 0:slot_count] = picked
        return carry

    if groups > 1:
        inputs[1].wait()
        lax.fori_loop(0, groups, gather, 0)
    else:
        gather(0, 0)

    inputs[2].wait()
    pair_band = pair_band_ref[...].reshape(1, half)
    source = lax.broadcasted_iota(jnp.int32, (half, half), 0)
    target = lax.broadcasted_iota(jnp.int32, (half, half), 1)
    earlier = jnp.where(source < target, 1.0, 0.0).astype(jnp.bfloat16)
    padded_bands = -(-bands // 16) * 16
    owner = lax.broadcasted_iota(jnp.int32, (padded_bands, half), 0) == pair_band
    counts = jnp.dot(
        jnp.where(owner, 1.0, 0.0).astype(jnp.bfloat16), earlier, preferred_element_type=jnp.float32
    )
    place = jnp.sum(jnp.where(owner, counts, 0.0), axis=0, keepdims=True)
    slot_of_pair = pair_band * slot_count + place.astype(jnp.int32)
    slot = lax.broadcasted_iota(jnp.int32, (padded, half), 0)
    hot = jnp.where(slot == slot_of_pair, 1.0, 0.0).astype(jnp.bfloat16)
    number = lax.broadcasted_iota(jnp.int32, (half, 2 * LANES), 0) + 1
    upper = lax.broadcasted_iota(jnp.int32, (half, 2 * LANES), 1) < LANES
    digits = jnp.where(upper, number // 8, lax.rem(number, 8)).astype(jnp.float32)
    found = jnp.dot(hot, digits.astype(jnp.bfloat16), preferred_element_type=jnp.float32)
    wave_column[...] = found[:, :LANES] * 8.0 + found[:, LANES:]
    number = lax.broadcasted_iota(jnp.int32, (16, half), 1) + 1
    upper = lax.broadcasted_iota(jnp.int32, (16, half), 0) < 8
    digits = jnp.where(upper, number // 8, lax.rem(number, 8)).astype(jnp.float32)
    found = lax.dot_general(
        digits.astype(jnp.bfloat16),
        hot,
        (((1,), (1,)), ((), ())),
        preferred_element_type=jnp.float32,
    )
    ordinal = found[0:8] * 8.0 + found[8:16]
    wave_row = jnp.concatenate([ordinal - 1.0, waves - ordinal], axis=1)
    held_row = jnp.concatenate([ordinal, ordinal], axis=1) > 0.0

    inputs[3].wait()

    def length_of(i):
        row = jnp.minimum(lane * rows + i, band_rows - 1)
        n = cycle_ref[latitude_ref[band * band_rows + row]]
        length = jnp.full((1, 1), n, jnp.int32).astype(jnp.float32)
        return row, n, length, 1.0 / length

    def prepare_steps(i):
        row, n, length, inverse = length_of(i)
        step_ref[i, 0], step_ref[i, 1] = cos_sin(wave_row * float(CHUNK), length, inverse)
        step_ref[i, 2], step_ref[i, 3] = cos_sin(wave_row * float(2 * CHUNK), length, inverse)
        kept = jnp.where(held_row & (2.0 * wave_row < length), 1.0, 0.0)
        weight_ref[i] = kept

    def prepare_table(i):
        row, n, length, inverse = length_of(i)

        def block(step, carry):
            start = pl.multiple_of(step * 16, 16)
            ordinal = wave_column[pl.ds(start, 16), :]
            for member in range(2):
                wave = ordinal - 1.0 if member == 0 else waves - ordinal
                for side in range(CHUNK // LANES):
                    place = lax.broadcasted_iota(jnp.int32, (16, LANES), 1) + side * LANES
                    cosine, sine = cos_sin(wave * place.astype(jnp.float32), length, inverse)
                    at = pl.ds(member * padded + start, 16)
                    columns = slice(side * LANES, (side + 1) * LANES)
                    table[i, at, columns] = cosine.astype(jnp.bfloat16)
                    at = pl.ds(width + member * padded + start, 16)
                    table[i, at, columns] = (-sine).astype(jnp.bfloat16)
            return carry

        lax.fori_loop(0, padded // 16, block, 0)

    prepare_steps(0)
    prepare_table(0)
    inputs[4].wait()
    inputs[5].wait()

    pl.semaphore_wait(barrier, devices - 1)
    send_chunks(leaving, arrived, send_sem, recv_sem, True)
    for j in range(1, lanes):
        factor_copy(j).start()
    cycles[:, block_of(lane)] = factor_ref[...]

    for i in range(1, rows):
        prepare_steps(i)
        prepare_table(i)
    for j in range(1, lanes):
        factor_copy(j).wait()
    for i in range(rows):
        chosen = lax.broadcasted_iota(jnp.int32, (band_rows, 1), 0) == length_of(i)[0]
        row_factor[i] = jnp.sum(
            jnp.where(chosen, cycles[...].astype(jnp.float32), 0.0), axis=0, keepdims=True
        )

    wait_chunks(leaving, arrived, send_sem, recv_sem)

    lane_index = lax.broadcasted_iota(jnp.int32, (stacked, LANES), 1)
    pieces = []
    for b in range(bands):
        piece = arrived[b * lanes : (b + 1) * lanes].astype(jnp.float32)
        pieces.append(piece.reshape(stacked, LANES).astype(jnp.bfloat16))
    by_part = jnp.dot(
        order_ref[...], jnp.concatenate(pieces, axis=1), preferred_element_type=jnp.float32
    )
    columns = [None] * (padded // LANES)
    for b in range(bands):
        first = b * slot_count
        turn = first % LANES
        piece = by_part[:, b * LANES : (b + 1) * LANES]
        piece = pltpu.roll(piece, turn, 1) if turn else piece
        for v in range(first // LANES, (first + slot_count - 1) // LANES + 1):
            begin = first - v * LANES
            if columns[v] is None:
                columns[v] = piece
            else:
                columns[v] = jnp.where(lane_index >= begin, piece, columns[v])
    columns = [jnp.zeros((stacked, LANES), jnp.float32) if c is None else c for c in columns]
    compact = jnp.concatenate(columns, axis=1)
    first_wave = jnp.where(wave_row == 0.0, 1.0, 2.0)

    def tall(value, count):
        return jnp.concatenate([value] * (count // 8), axis=0)

    def part_of(member, t, i):
        return ((member * 2 + t) * rows + i) * fields

    for i in range(rows):
        row, n, length, inverse = length_of(i)
        norm = lax.rsqrt(length)
        live = tall(weight_ref[i] > 0.0, fields)
        scale = tall(first_wave, fields)
        state = []
        for t in range(2):
            held = jnp.concatenate(
                [compact[part_of(m, t, i) : part_of(m, t, i) + fields] for m in range(2)], axis=1
            )
            state.append(jnp.where(live, held * scale, 0.0))
        real, imag = state
        cosine, sine = tall(step_ref[i, 0], fields), tall(step_ref[i, 1], fields)
        real, imag = (
            jnp.concatenate([real, real * cosine - imag * sine], axis=0),
            jnp.concatenate([imag, real * sine + imag * cosine], axis=0),
        )
        cosine, sine = tall(step_ref[i, 2], 2 * fields), tall(step_ref[i, 3], 2 * fields)
        for h in range(chunks // 2):
            at = slice(2 * h * fields, 2 * (h + 1) * fields)
            lhs[i, at, 0:width] = real.astype(jnp.bfloat16)
            lhs[i, at, width : 2 * width] = imag.astype(jnp.bfloat16)
            if h < chunks // 2 - 1:
                real, imag = real * cosine - imag * sine, real * sine + imag * cosine

    for i in range(rows):
        row, n, length, inverse = length_of(i)
        norm = lax.rsqrt(length)
        found = jnp.dot(lhs[i], table[i], preferred_element_type=jnp.float32)
        for h in range(0, chunks, 2):
            pair = []
            for g in (h, h + 1):
                at = g * CHUNK + lax.broadcasted_iota(jnp.int32, (1, CHUNK), 1)
                value = found[g * fields : (g + 1) * fields]
                value = jnp.where(at < n, value * norm, 0.0).astype(jnp.bfloat16)
                grid_ref[i, :, g * CHUNK : (g + 1) * CHUNK] = value
                factor = row_factor[i, :, g * CHUNK : (g + 1) * CHUNK]
                pair.append(factor * value.astype(jnp.float32))
            product_ref[i, h * fields : (h + 2) * fields, :] = jnp.concatenate(
                pair, axis=0
            ).astype(jnp.bfloat16)
        for j in range(1, lanes):
            grid_copy(i, j).start()
        blocks[lane, i] = grid_ref[i, :, block_of(lane)]

    for i in range(rows):
        row, n, length, inverse = length_of(i)
        norm = lax.rsqrt(length)
        left = product_ref[i]
        for c in range(width // CHUNK):
            columns = slice(c * CHUNK, (c + 1) * CHUNK)
            parts_found = []
            for t in range(2):
                right = table[i, t * width + c * CHUNK : t * width + (c + 1) * CHUNK, :]
                parts_found.append(
                    lax.dot_general(
                        left, right, (((1,), (1,)), ((), ())), preferred_element_type=jnp.float32
                    )
                )
            cosine = tall(step_ref[i, 0, :, columns], fields)
            sine = tall(step_ref[i, 1, :, columns], fields)
            last = slice((chunks - 1) * fields, chunks * fields)
            real, imag = parts_found[0][last], parts_found[1][last]
            for h in range(chunks - 2, -1, -1):
                at = slice(h * fields, (h + 1) * fields)
                real, imag = (
                    real * cosine + imag * sine + parts_found[0][at],
                    imag * cosine - real * sine + parts_found[1][at],
                )
            scale = tall(weight_ref[i, :, columns], fields) * norm
            for t, value in ((0, real), (1, imag)):
                at = pl.ds((t * rows + i) * fields, fields)
                finished[at, columns] = value * scale

    spread = []
    for b in range(bands):
        first = b * slot_count
        turn = first % LANES
        v = first // LANES
        members = []
        for member in range(2):
            base = member * padded + v * LANES
            piece = finished[:, base : base + LANES]
            piece = pltpu.roll(piece, LANES - turn, 1) if turn else piece
            if turn + slot_count > LANES:
                after = pltpu.roll(finished[:, base + LANES : base + 2 * LANES], LANES - turn, 1)
                piece = jnp.where(lane_index[: piece.shape[0]] < LANES - turn, piece, after)
            members.append(piece)
        spread.append(jnp.concatenate(members, axis=0).astype(jnp.bfloat16))
    by_lane = lax.dot_general(
        order_ref[...],
        jnp.concatenate(spread, axis=1),
        (((0,), (0,)), ((), ())),
        preferred_element_type=jnp.float32,
    )
    for b in range(bands):
        piece = by_lane[:, b * LANES : (b + 1) * LANES].reshape(lanes, chunk_rows, LANES)
        result[b * lanes : (b + 1) * lanes] = piece.astype(jnp.bfloat16)

    send_chunks(result, returned, back_send_sem, back_recv_sem, False)
    for i in range(rows):
        for j in range(1, lanes):
            grid_copy(i, j).wait()
    wait_chunks(result, returned, back_send_sem, back_recv_sem)

    def place_group(group):
        held = returned[devices_of(group)].astype(jnp.float32)
        held = held.reshape(GROUP * entry, LANES).astype(jnp.bfloat16)
        return lax.dot_general(
            pick[...], held, (((0,), (0,)), ((), ())), preferred_element_type=jnp.float32
        )

    if groups == 1:
        placed = place_group(0)
    else:

        def add(group, total):
            fill_pick(group)
            return total + place_group(group)

        placed = lax.fori_loop(0, groups, add, jnp.zeros((size, LANES), jnp.float32))
    placed = placed[:, :slot_count].reshape(own_fields, parts, latitudes, slot_count)
    tendencies[...] = placed.astype(jnp.bfloat16)


def round_trip(coefficients, cycle_length, row_latitude, pair_band, factor, order, bands, lanes):
    devices = bands * lanes
    own_fields, parts, latitudes, slot_count = coefficients.shape
    fields = own_fields * lanes
    band_rows, points = factor.shape
    rows = -(-band_rows // lanes)
    entry = parts * own_fields
    padded = -(-bands * slot_count // LANES) * LANES
    width = 2 * padded
    chunks = lanes * points // CHUNK
    exchange = (devices, rows * entry, LANES)
    bf16, f32 = jnp.bfloat16, jnp.float32
    hbm = pl.BlockSpec(memory_space=pltpu.MemorySpace.HBM)
    return pl.pallas_call(
        functools.partial(round_kernel, bands, lanes),
        in_specs=[hbm] * 6,
        out_specs=[pl.BlockSpec(memory_space=pltpu.VMEM)] * 2,
        scratch_shapes=[
            pltpu.VMEM(coefficients.shape, bf16),
            pltpu.SMEM(cycle_length.shape, jnp.int32),
            pltpu.SMEM(row_latitude.shape, jnp.int32),
            pltpu.VMEM(pair_band.shape, jnp.int32),
            pltpu.VMEM(factor.shape, bf16),
            pltpu.VMEM(order.shape, bf16),
            pltpu.VMEM((GROUP * entry, latitudes * entry), bf16),
            pltpu.VMEM(exchange, bf16),
            pltpu.VMEM(exchange, bf16),
            pltpu.VMEM(exchange, bf16),
            pltpu.VMEM(exchange, bf16),
            pltpu.VMEM((band_rows, lanes * points), bf16),
            pltpu.VMEM((rows, fields, lanes * points), bf16),
            pltpu.VMEM((rows, 2 * width, CHUNK), bf16),
            pltpu.VMEM((rows, chunks * fields, 2 * width), bf16),
            pltpu.VMEM((rows, chunks * fields, CHUNK), bf16),
            pltpu.VMEM((rows, 1, lanes * points), f32),
            pltpu.VMEM((padded, LANES), f32),
            pltpu.VMEM((rows, 4, 8, width), f32),
            pltpu.VMEM((rows, 8, width), f32),
            pltpu.VMEM((2 * rows * fields, width), f32),
        ]
        + [pltpu.SemaphoreType.DMA((6,))]
        + [pltpu.SemaphoreType.DMA] * 4
        + [pltpu.SemaphoreType.DMA((lanes,))] * 2
        + [pltpu.SemaphoreType.DMA((rows, lanes))] * 2,
        out_shape=[
            jax.ShapeDtypeStruct((lanes, rows, fields, points), bf16),
            jax.ShapeDtypeStruct(coefficients.shape, bf16),
        ],
        compiler_params=pltpu.CompilerParams(
            collective_id=0, has_side_effects=True, vmem_limit_bytes=40 << 20
        ),
    )(
        *[
            pltpu.with_memory_space_constraint(array, pltpu.MemorySpace.HBM)
            for array in (coefficients, cycle_length, row_latitude, pair_band, factor, order)
        ]
    )


def on_device(coefficients, cycle_length, row_latitude, pair_band, gridpoint_factor):
    bands, lanes = lax.axis_size("band"), lax.axis_size("lon")
    own_fields, slot_count, parts, latitudes = coefficients.shape
    band_rows, points = gridpoint_factor.shape
    fields = own_fields * lanes
    own_rows = -(-band_rows // lanes)
    stacked = lanes * own_rows * parts * own_fields
    places = np.arange(stacked).reshape(lanes, own_rows, parts, own_fields)
    places = places.transpose(2, 1, 0, 3).reshape(-1)
    order = jnp.asarray(places[:, None] == np.arange(stacked)[None, :], dtype=jnp.bfloat16)
    blocks, placed = round_trip(
        jnp.transpose(coefficients, (0, 2, 3, 1)),
        cycle_length,
        row_latitude,
        pair_band,
        gridpoint_factor,
        order,
        bands,
        lanes,
    )
    grid_rows = blocks.reshape(lanes * own_rows, fields, points)[:band_rows]
    return (jnp.transpose(grid_rows, (1, 0, 2)), jnp.transpose(placed, (0, 3, 1, 2)))


def solution(mesh):
    return jax.shard_map(
        on_device,
        mesh=mesh,
        in_specs=(P("lon", "band", None, None), P(), P(), P(), P("band", "lon")),
        out_specs=(P(None, "band", "lon"), P("lon", "band", None, None)),
        check_vma=False,
    )
```

time: 29.9 us -> 23.9 us (0.80)
  Pallas kernels: 24.8 us -> 21.7 us
  local copies, waits for them, and re-layouts: 3.21 us -> 1.35 us
  matrix products: 1.04 us -> 0 us
    pallas_call x1, Pallas kernels: 24.8 us -> 21.7 us  [round_trip(): pl.pallas_call(functools.partial(round_kernel, bands, lanes), in_specs=[h...]
    unnamed x14 -> x1, local copies, waits for them, and re-layouts: 2.38 us -> 0.65 us
    dot_general x2 -> x0, matrix products: 1.04 us -> none  [the longest x1 0.88 us: on_device(): jnp.einsum('rl,fstl->rtfs', onehot.astype(jnp.bfloat16), coefficients, pr...]
where the time goes in v1:
time: 23.9 us; the launch traced here: 23.7 us
  Pallas kernels  21.7 us (91%)
  local copies, waits for them, and re-layouts  1.35 us (6%)
  between operations  0.64 us (3%)
    pallas_call x1, Pallas kernels, round_trip(): pl.pallas_call(functools.partial(round_kernel, bands, lanes), in_specs=[h...  21.7 us
    reshape x1, local copies, waits for them, and re-layouts, on_device(): grid_rows = blocks.reshape(lanes * own_rows, fields, points)[:band_rows]  0.69 us
    unnamed x1, local copies, waits for them, and re-layouts  0.65 us

profile of v1, /device:TPU:0, one launch (start us, length us, event | category | flops | bytes accessed | tf_op | source)
XLA Modules:
  0.0 23.7 jit_solution(13392291650503800433)
XLA Ops:
  0.6 21.7 %shard_map.77 = (bf16[4,2,8,1408]{3,2,1,0:T(8,128)(2,1)S(1)}, bf16[2,4,64,80]{3,2,1,0:T(8,128)(2,1)S(1)}) custom-call(bf16[2,4,64,80]{3,2,1,0:T(8,128)(2,1)} %bitcast.9, s32[64]{0:T(128)} %cycle_hbm.1, s32[64]{0:T(128)} %latitude_hbm.1, s32[640]{0:T(1024)} %pair_band_hbm.1, bf16[8,1408]{1,0:T(8,128)(2,1)} %factor_hbm.1, bf16[64,64]{1,0:T(8,128)(2,1)} %constant.2.clone.order_hbm), custom_call_target="tpu_custom_call" | custom-call | tf_op jit(solution)/shard_map/pallas_call | solution.py:478
  22.4 0.7 %copy.10 = bf16[8,8,1408]{2,0,1:T(8,128)(2,1)} copy(bf16[8,8,1408]{2,1,0:T(8,128)(2,1)S(1)} %bitcast.6) | data formatting | bytes 360448 | tf_op jit(solution)/shard_map/reshape | solution.py:544
  23.0 0.7 %copy.12 = bf16[2,80,4,64]{1,3,2,0:T(8,128)(2,1)} copy(bf16[2,80,4,64]{1,3,2,0:T(8,128)(2,1)S(1)} %bitcast.7) | data formatting | bytes 163840

commit v2 on v1

--- a/solution.py
+++ b/solution.py
@@ -14,6 +14,7 @@
 CHUNK = 256
 GROUP = 64
 MESH = pl.DeviceIdType.MESH
+LOGICAL = pl.DeviceIdType.LOGICAL
 
 
 def cos_sin(product, length, inverse):
@@ -86,39 +87,66 @@
     chunks = cycle_points // CHUNK
     entry = parts * own_fields
     entries = devices * rows
-    chunk_rows = rows * entry
-    stacked = chunk_rows * lanes
+    stacked = entry * lanes
     groups = entries // GROUP
-    group_devices = GROUP // rows
+    every = slice(0, rows)
     unroll = devices <= 32
 
-    def peer(k):
-        flat = lax.rem(me + k, devices)
-        return flat, {"band": flat // lanes, "lon": lax.rem(flat, lanes)}
+    plane = 2 * lanes
+    planes = devices // plane
+    own_plane = lax.div(band, 2)
+    own_place = me - own_plane * plane
+    upper_half = own_plane >= planes - planes // 2
+
+    def for_peers(act, first_planes):
+        def place_at(turn):
+            place = own_place + turn
+            return jnp.where(place >= plane, place - plane, place)
+
+        def facing(shift):
+            level = own_plane + shift
+            level = jnp.where(level >= planes, level - planes, level)
+            act(level * plane + own_place)
+
+        def others(step, turn):
+            level = jnp.where(first_planes, step, planes - 1 - step)
+            act(level * plane + place_at(turn))
+
+        if unroll:
+            for shift in range(1, planes):
+                facing(shift)
+            for step in range(planes):
+                for turn in range(1, plane):
+                    others(step, turn)
+        else:
+            lax.fori_loop(1, planes, lambda shift, carry: (facing(shift), carry)[1], 0)
+
+            def one(step, carry):
+                return lax.fori_loop(1, plane, lambda turn, c: (others(step, turn), c)[1], carry)
+
+            lax.fori_loop(0, planes, one, 0)
 
     def block_of(index):
         return pl.ds(pl.multiple_of(index * points, LANES), points)
 
-    def send_chunks(source, target, sent, received, far_first):
-        def send(k, carry):
-            flat, device = peer(devices - k if far_first else k)
+    def send_chunks(source, target, sent, received, row, first_planes):
+        def send(flat):
             pltpu.make_async_remote_copy(
-                src_ref=source.at[flat],
-                dst_ref=target.at[me],
+                src_ref=source.at[row, flat],
+                dst_ref=target.at[row, me],
                 send_sem=sent,
                 recv_sem=received,
-                device_id=device,
-                device_id_type=MESH,
+                device_id=flat,
+                device_id_type=LOGICAL,
             ).start()
-            return carry
-
-        lax.fori_loop(1, devices, send, 0, unroll=unroll)
-        target[me] = source[me]
-
-    def wait_chunks(source, target, sent, received):
+
+        for_peers(send, first_planes)
+        target[row, me] = source[row, me]
+
+    def wait_chunks(source, target, sent, received, row):
         pltpu.make_async_remote_copy(
-            src_ref=source.at[pl.ds(0, devices - 1)],
-            dst_ref=target.at[pl.ds(0, devices - 1)],
+            src_ref=source.at[row, pl.ds(0, devices - 1)],
+            dst_ref=target.at[row, pl.ds(0, devices - 1)],
             send_sem=sent,
             recv_sem=received,
             device_id={"band": band, "lon": lane},
@@ -148,9 +176,8 @@
 
     barrier = pltpu.get_barrier_semaphore()
 
-    def signal(k, carry):
-        pl.semaphore_signal(barrier, inc=1, device_id=peer(k)[1], device_id_type=MESH)
-        return carry
+    def signal(flat):
+        pl.semaphore_signal(barrier, inc=1, device_id=flat, device_id_type=LOGICAL)
 
     inputs = [
         pltpu.make_async_copy(source, target, input_sem.at[index])
@@ -165,7 +192,7 @@
             )
         )
     ]
-    lax.fori_loop(1, devices, signal, 0, unroll=unroll)
+    for_peers(signal, upper_half)
     for copy in inputs:
         copy.start()
 
@@ -179,19 +206,20 @@
             pieces = []
             for side in range(2):
                 number = group * GROUP + pair * 2 + side
-                device, i = number // rows, lax.rem(number, rows)
-                local = lax.rem(device, lanes) * rows + i
-                row = (device // lanes) * band_rows + jnp.minimum(local, band_rows - 1)
-                held = jnp.where(local < band_rows, latitude_ref[row], -(1 << 20))
+                if band_rows == lanes * rows:
+                    i, device = lax.div(number, devices), lax.rem(number, devices)
+                    held = latitude_ref[device * rows + i]
+                else:
+                    i, device = lax.div(number, devices), lax.rem(number, devices)
+                    local = lax.rem(device, lanes) * rows + i
+                    row = (device // lanes) * band_rows + jnp.minimum(local, band_rows - 1)
+                    held = jnp.where(local < band_rows, latitude_ref[row], -(1 << 20))
                 pieces.append(jnp.where(latitude_of == held, 1.0, 0.0))
             start = pl.multiple_of(pair * 2 * entry, 2 * entry)
             pick[pl.ds(start, 2 * entry), :] = jnp.concatenate(pieces, axis=0).astype(jnp.bfloat16)
             return carry
 
         lax.fori_loop(0, GROUP // 2, one, 0, unroll=4)
-
-    def devices_of(group):
-        return pl.ds(group * group_devices, group_devices)
 
     leaving[...] = jnp.zeros_like(leaving)
     inputs[0].wait()
@@ -206,8 +234,12 @@
         picked = jnp.dot(
             pick[...], inputs_ready.reshape(size, slot_count), preferred_element_type=jnp.float32
         )
-        picked = picked.reshape(group_devices, chunk_rows, slot_count).astype(jnp.bfloat16)
-        leaving[devices_of(group), :, 0:slot_count] = picked
+        if groups > 1:
+            picked = picked.reshape(GROUP, entry, slot_count).astype(jnp.bfloat16)
+            leaving[0, pl.ds(group * GROUP, GROUP), :, 0:slot_count] = picked
+        else:
+            picked = picked.reshape(rows, devices, entry, slot_count).astype(jnp.bfloat16)
+            leaving[:, :, :, 0:slot_count] = picked
         return carry
 
     if groups > 1:
@@ -250,6 +282,9 @@
 
     inputs[3].wait()
 
+    def tall(value, count):
+        return jnp.concatenate([value] * (count // 8), axis=0)
+
     def length_of(i):
         row = jnp.minimum(lane * rows + i, band_rows - 1)
         n = cycle_ref[latitude_ref[band * band_rows + row]]
@@ -263,40 +298,56 @@
         kept = jnp.where(held_row & (2.0 * wave_row < length), 1.0, 0.0)
         weight_ref[i] = kept
 
-    def prepare_table(i):
+    def prepare_table(i, begin, end):
         row, n, length, inverse = length_of(i)
+
+        places = lax.broadcasted_iota(jnp.int32, (8, CHUNK), 1).astype(jnp.float32)
+        last_cosine, last_sine = cos_sin(places * float(waves - 1), length, inverse)
 
         def block(step, carry):
             start = pl.multiple_of(step * 16, 16)
             ordinal = wave_column[pl.ds(start, 16), :]
-            for member in range(2):
-                wave = ordinal - 1.0 if member == 0 else waves - ordinal
-                for side in range(CHUNK // LANES):
-                    place = lax.broadcasted_iota(jnp.int32, (16, LANES), 1) + side * LANES
-                    cosine, sine = cos_sin(wave * place.astype(jnp.float32), length, inverse)
+            for side in range(CHUNK // LANES):
+                columns = slice(side * LANES, (side + 1) * LANES)
+                place = lax.broadcasted_iota(jnp.int32, (16, LANES), 1) + side * LANES
+                product = (ordinal - 1.0) * place.astype(jnp.float32)
+                cosine, sine = cos_sin(product, length, inverse)
+                top_cosine = tall(last_cosine[:, columns], 16)
+                top_sine = tall(last_sine[:, columns], 16)
+                pairs = (
+                    (cosine, sine),
+                    (
+                        top_cosine * cosine + top_sine * sine,
+                        top_sine * cosine - top_cosine * sine,
+                    ),
+                )
+                for member, (cosine, sine) in enumerate(pairs):
                     at = pl.ds(member * padded + start, 16)
-                    columns = slice(side * LANES, (side + 1) * LANES)
                     table[i, at, columns] = cosine.astype(jnp.bfloat16)
                     at = pl.ds(width + member * padded + start, 16)
                     table[i, at, columns] = (-sine).astype(jnp.bfloat16)
             return carry
 
-        lax.fori_loop(0, padded // 16, block, 0)
-
-    prepare_steps(0)
-    prepare_table(0)
+        lax.fori_loop(begin, end, block, 0)
+
+    blocks_all = padded // 16
+    quarter = lax.div(own_plane * 4, planes)
+    early = [jnp.where(quarter == 3, blocks_all // 2, blocks_all)]
+    early += [jnp.where(quarter == 0, blocks_all, 0)] * (rows - 1)
+    for i in range(rows):
+        prepare_table(i, 0, early[i])
     inputs[4].wait()
     inputs[5].wait()
 
     pl.semaphore_wait(barrier, devices - 1)
-    send_chunks(leaving, arrived, send_sem, recv_sem, True)
+    send_chunks(leaving, arrived, send_sem, recv_sem, every, upper_half)
     for j in range(1, lanes):
         factor_copy(j).start()
     cycles[:, block_of(lane)] = factor_ref[...]
 
-    for i in range(1, rows):
+    for i in range(rows):
         prepare_steps(i)
-        prepare_table(i)
+        prepare_table(i, early[i], blocks_all)
     for j in range(1, lanes):
         factor_copy(j).wait()
     for i in range(rows):
@@ -305,37 +356,35 @@
             jnp.where(chosen, cycles[...].astype(jnp.float32), 0.0), axis=0, keepdims=True
         )
 
-    wait_chunks(leaving, arrived, send_sem, recv_sem)
+    wait_chunks(leaving, arrived, send_sem, recv_sem, every)
 
     lane_index = lax.broadcasted_iota(jnp.int32, (stacked, LANES), 1)
-    pieces = []
-    for b in range(bands):
-        piece = arrived[b * lanes : (b + 1) * lanes].astype(jnp.float32)
-        pieces.append(piece.reshape(stacked, LANES).astype(jnp.bfloat16))
-    by_part = jnp.dot(
-        order_ref[...], jnp.concatenate(pieces, axis=1), preferred_element_type=jnp.float32
-    )
-    columns = [None] * (padded // LANES)
-    for b in range(bands):
-        first = b * slot_count
-        turn = first % LANES
-        piece = by_part[:, b * LANES : (b + 1) * LANES]
-        piece = pltpu.roll(piece, turn, 1) if turn else piece
-        for v in range(first // LANES, (first + slot_count - 1) // LANES + 1):
-            begin = first - v * LANES
-            if columns[v] is None:
-                columns[v] = piece
-            else:
-                columns[v] = jnp.where(lane_index >= begin, piece, columns[v])
-    columns = [jnp.zeros((stacked, LANES), jnp.float32) if c is None else c for c in columns]
-    compact = jnp.concatenate(columns, axis=1)
+    def compact_of(i):
+        pieces = []
+        for b in range(bands):
+            piece = arrived[i, b * lanes : (b + 1) * lanes].astype(jnp.float32)
+            pieces.append(piece.reshape(stacked, LANES).astype(jnp.bfloat16))
+        by_part = jnp.dot(
+            order_ref[...], jnp.concatenate(pieces, axis=1), preferred_element_type=jnp.float32
+        )
+        columns = [jnp.zeros((stacked, LANES), jnp.float32)] * (padded // LANES)
+        for b in range(bands):
+            first = b * slot_count
+            turn = first % LANES
+            piece = by_part[:, b * LANES : (b + 1) * LANES]
+            piece = pltpu.roll(piece, turn, 1) if turn else piece
+            for v in range(first // LANES, (first + slot_count - 1) // LANES + 1):
+                begin = first - v * LANES
+                if begin <= 0:
+                    columns[v] = piece
+                else:
+                    columns[v] = jnp.where(lane_index >= begin, piece, columns[v])
+        return jnp.concatenate(columns, axis=1)
+
     first_wave = jnp.where(wave_row == 0.0, 1.0, 2.0)
 
-    def tall(value, count):
-        return jnp.concatenate([value] * (count // 8), axis=0)
-
-    def part_of(member, t, i):
-        return ((member * 2 + t) * rows + i) * fields
+    def part_of(member, t):
+        return (member * 2 + t) * fields
 
     for i in range(rows):
         row, n, length, inverse = length_of(i)
@@ -343,9 +392,10 @@
         live = tall(weight_ref[i] > 0.0, fields)
         scale = tall(first_wave, fields)
         state = []
+        compact = compact_of(i)
         for t in range(2):
             held = jnp.concatenate(
-                [compact[part_of(m, t, i) : part_of(m, t, i) + fields] for m in range(2)], axis=1
+                [compact[part_of(m, t) : part_of(m, t) + fields] for m in range(2)], axis=1
             )
             state.append(jnp.where(live, held * scale, 0.0))
         real, imag = state
@@ -381,6 +431,34 @@
         for j in range(1, lanes):
             grid_copy(i, j).start()
         blocks[lane, i] = grid_ref[i, :, block_of(lane)]
+
+    def finish_row(i):
+        spread = []
+        for b in range(bands):
+            first = b * slot_count
+            turn = first % LANES
+            v = first // LANES
+            members = []
+            for member in range(2):
+                base = member * padded + v * LANES
+                piece = finished[i, :, base : base + LANES]
+                piece = pltpu.roll(piece, LANES - turn, 1) if turn else piece
+                if turn + slot_count > LANES:
+                    after = finished[i, :, base + LANES : base + 2 * LANES]
+                    after = pltpu.roll(after, LANES - turn, 1)
+                    piece = jnp.where(lane_index[: 2 * fields] < LANES - turn, piece, after)
+                members.append(piece)
+            spread.append(jnp.concatenate(members, axis=0).astype(jnp.bfloat16))
+        by_lane = lax.dot_general(
+            order_ref[...],
+            jnp.concatenate(spread, axis=1),
+            (((0,), (0,)), ((), ())),
+            preferred_element_type=jnp.float32,
+        )
+        for b in range(bands):
+            piece = by_lane[:, b * LANES : (b + 1) * LANES].reshape(lanes, entry, LANES)
+            result[i, b * lanes : (b + 1) * lanes] = piece.astype(jnp.bfloat16)
+        send_chunks(result, returned, back_send_sem.at[i], back_recv_sem.at[i], i, True)
 
     for i in range(rows):
         row, n, length, inverse = length_of(i)
@@ -408,42 +486,20 @@
                 )
             scale = tall(weight_ref[i, :, columns], fields) * norm
             for t, value in ((0, real), (1, imag)):
-                at = pl.ds((t * rows + i) * fields, fields)
-                finished[at, columns] = value * scale
-
-    spread = []
-    for b in range(bands):
-        first = b * slot_count
-        turn = first % LANES
-        v = first // LANES
-        members = []
-        for member in range(2):
-            base = member * padded + v * LANES
-            piece = finished[:, base : base + LANES]
-            piece = pltpu.roll(piece, LANES - turn, 1) if turn else piece
-            if turn + slot_count > LANES:
-                after = pltpu.roll(finished[:, base + LANES : base + 2 * LANES], LANES - turn, 1)
-                piece = jnp.where(lane_index[: piece.shape[0]] < LANES - turn, piece, after)
-            members.append(piece)
-        spread.append(jnp.concatenate(members, axis=0).astype(jnp.bfloat16))
-    by_lane = lax.dot_general(
-        order_ref[...],
-        jnp.concatenate(spread, axis=1),
-        (((0,), (0,)), ((), ())),
-        preferred_element_type=jnp.float32,
-    )
-    for b in range(bands):
-        piece = by_lane[:, b * LANES : (b + 1) * LANES].reshape(lanes, chunk_rows, LANES)
-        result[b * lanes : (b + 1) * lanes] = piece.astype(jnp.bfloat16)
-
-    send_chunks(result, returned, back_send_sem, back_recv_sem, False)
+                finished[i, t * fields : (t + 1) * fields, columns] = value * scale
+        finish_row(i)
+
     for i in range(rows):
         for j in range(1, lanes):
             grid_copy(i, j).wait()
-    wait_chunks(result, returned, back_send_sem, back_recv_sem)
+    for i in range(rows):
+        wait_chunks(result, returned, back_send_sem.at[i], back_recv_sem.at[i], i)
 
     def place_group(group):
-        held = returned[devices_of(group)].astype(jnp.float32)
+        if groups > 1:
+            held = returned[0, pl.ds(group * GROUP, GROUP)].astype(jnp.float32)
+        else:
+            held = returned[...].astype(jnp.float32)
         held = held.reshape(GROUP * entry, LANES).astype(jnp.bfloat16)
         return lax.dot_general(
             pick[...], held, (((0,), (0,)), ((), ())), preferred_element_type=jnp.float32
@@ -472,7 +528,7 @@
     padded = -(-bands * slot_count // LANES) * LANES
     width = 2 * padded
     chunks = lanes * points // CHUNK
-    exchange = (devices, rows * entry, LANES)
+    exchange = (rows, devices, entry, LANES)
     bf16, f32 = jnp.bfloat16, jnp.float32
     hbm = pl.BlockSpec(memory_space=pltpu.MemorySpace.HBM)
     return pl.pallas_call(
@@ -500,10 +556,11 @@
             pltpu.VMEM((padded, LANES), f32),
             pltpu.VMEM((rows, 4, 8, width), f32),
             pltpu.VMEM((rows, 8, width), f32),
-            pltpu.VMEM((2 * rows * fields, width), f32),
+            pltpu.VMEM((rows, 2 * fields, width), f32),
         ]
         + [pltpu.SemaphoreType.DMA((6,))]
-        + [pltpu.SemaphoreType.DMA] * 4
+        + [pltpu.SemaphoreType.DMA] * 2
+        + [pltpu.SemaphoreType.DMA((rows,))] * 2
         + [pltpu.SemaphoreType.DMA((lanes,))] * 2
         + [pltpu.SemaphoreType.DMA((rows, lanes))] * 2,
         out_shape=[
@@ -521,15 +578,43 @@
     )
 
 
+def place_kernel(blocks, placed, grid_out, tendencies_out, grid_ref, sem):
+    tendencies_copy = pltpu.make_async_copy(placed, tendencies_out, sem.at[0])
+    tendencies_copy.start()
+    lanes, rows, fields, points = blocks.shape
+    held = blocks[...].astype(jnp.float32).reshape(lanes * rows, fields, points)
+    grid_ref[...] = jnp.swapaxes(held, 0, 1).astype(jnp.bfloat16)
+    grid_copy = pltpu.make_async_copy(grid_ref, grid_out, sem.at[1])
+    grid_copy.start()
+    tendencies_copy.wait()
+    grid_copy.wait()
+
+
+def place_outputs(blocks, placed):
+    lanes, rows, fields, points = blocks.shape
+    grid_shape = (fields, lanes * rows, points)
+    return pl.pallas_call(
+        place_kernel,
+        in_specs=[pl.BlockSpec(memory_space=pltpu.VMEM)] * 2,
+        out_specs=[pl.BlockSpec(memory_space=pl.ANY)] * 2,
+        out_shape=[
+            jax.ShapeDtypeStruct(grid_shape, jnp.bfloat16),
+            jax.ShapeDtypeStruct(placed.shape, jnp.bfloat16),
+        ],
+        scratch_shapes=[pltpu.VMEM(grid_shape, jnp.bfloat16), pltpu.SemaphoreType.DMA((2,))],
+        compiler_params=pltpu.CompilerParams(vmem_limit_bytes=16 << 20),
+    )(blocks, placed)
+
+
 def on_device(coefficients, cycle_length, row_latitude, pair_band, gridpoint_factor):
     bands, lanes = lax.axis_size("band"), lax.axis_size("lon")
     own_fields, slot_count, parts, latitudes = coefficients.shape
     band_rows, points = gridpoint_factor.shape
     fields = own_fields * lanes
     own_rows = -(-band_rows // lanes)
-    stacked = lanes * own_rows * parts * own_fields
-    places = np.arange(stacked).reshape(lanes, own_rows, parts, own_fields)
-    places = places.transpose(2, 1, 0, 3).reshape(-1)
+    stacked = lanes * parts * own_fields
+    places = np.arange(stacked).reshape(lanes, parts, own_fields)
+    places = places.transpose(1, 0, 2).reshape(-1)
     order = jnp.asarray(places[:, None] == np.arange(stacked)[None, :], dtype=jnp.bfloat16)
     blocks, placed = round_trip(
         jnp.transpose(coefficients, (0, 2, 3, 1)),
@@ -541,6 +626,9 @@
         bands,
         lanes,
     )
+    if lanes * own_rows == band_rows and band_rows % 8 == 0 and fields % 8 == 0:
+        grid, placed = place_outputs(blocks, placed)
+        return (grid, jnp.transpose(placed, (0, 3, 1, 2)))
     grid_rows = blocks.reshape(lanes * own_rows, fields, points)[:band_rows]
     return (jnp.transpose(grid_rows, (1, 0, 2)), jnp.transpose(placed, (0, 3, 1, 2)))
 

time: 23.9 us -> 22.8 us (0.954)
  local copies, waits for them, and re-layouts: 1.35 us -> 0 us
  Pallas kernels: 21.7 us -> 22 us
    pallas_call x0 -> x1, Pallas kernels: none -> 0.78 us  [place_outputs(): pl.pallas_call(place_kernel, in_specs=[pl.BlockSpec(memory_space=pltpu.VM...]
    reshape x1 -> x0, local copies, waits for them, and re-layouts: 0.69 us -> none  [on_device(): grid_rows = blocks.reshape(lanes * own_rows, fields, points)[:band_rows]]
    unnamed x1 -> x0, local copies, waits for them, and re-layouts: 0.65 us -> none
    pallas_call x1, Pallas kernels: 21.7 us -> 21.2 us  [round_trip(): pl.pallas_call(functools.partial(round_kernel, bands, lanes), in_specs=[h...]
where the time goes in v2:
time: 22.8 us; the launch traced here: 22.7 us
  Pallas kernels  22 us (96%)
  between operations  0.64 us (3%)
    pallas_call x1, Pallas kernels, round_trip(): pl.pallas_call(functools.partial(round_kernel, bands, lanes), in_specs=[h...  21.2 us
    pallas_call x1, Pallas kernels, place_outputs(): pl.pallas_call(place_kernel, in_specs=[pl.BlockSpec(memory_space=pltpu.VM...  0.78 us

profile of v2, /device:TPU:0, one launch (start us, length us, event | category | flops | bytes accessed | tf_op | source)
XLA Modules:
  0.0 22.7 jit_solution(17944694609074598006)
XLA Ops:
  0.6 21.2 %shard_map.77 = (bf16[4,2,8,1408]{3,2,1,0:T(8,128)(2,1)S(1)}, bf16[2,4,64,80]{3,2,1,0:T(8,128)(2,1)S(1)}) custom-call(bf16[2,4,64,80]{3,2,1,0:T(8,128)(2,1)} %bitcast.2, s32[64]{0:T(128)} %cycle_hbm.1, s32[64]{0:T(128)} %latitude_hbm.1, s32[640]{0:T(1024)} %pair_band_hbm.1, bf16[8,1408]{1,0:T(8,128)(2,1)} %factor_hbm.1, bf16[32,32]{1,0:T(8,128)(2,1)} %constant.2.clone.order_hbm), custom_call_target="tpu_custom_call" | custom-call | tf_op jit(solution)/shard_map/pallas_call | solution.py:534
  21.9 0.8 %shard_map.78 = (bf16[8,8,1408]{2,1,0:T(8,128)(2,1)}, bf16[2,4,64,80]{3,2,1,0:T(8,128)(2,1)}) custom-call(bf16[4,2,8,1408]{3,2,1,0:T(8,128)(2,1)S(1)} %get-tuple-element.6.blocks, bf16[2,4,64,80]{3,2,1,0:T(8,128)(2,1)S(1)} %get-tuple-element.7.placed), custom_call_target="tpu_custom_call" | custom-call | tf_op jit(solution)/shard_map/pallas_call | solution.py:596

commit v3 on v2

--- a/solution.py
+++ b/solution.py
@@ -40,8 +40,9 @@
     pair_band_hbm,
     factor_hbm,
     order_hbm,
+    grid_out,
+    tendencies,
     blocks,
-    tendencies,
     coefficients,
     cycle_ref,
     latitude_ref,
@@ -90,6 +91,9 @@
     stacked = entry * lanes
     groups = entries // GROUP
     every = slice(0, rows)
+    main, rest = LANES // 2, LANES // 8
+    packed = bands == 8 and entry == 8 and groups == 1 and main < slot_count <= main + rest
+    wire = slice(0, 6) if packed else slice(0, entry)
     unroll = devices <= 32
 
     plane = 2 * lanes
@@ -132,8 +136,8 @@
     def send_chunks(source, target, sent, received, row, first_planes):
         def send(flat):
             pltpu.make_async_remote_copy(
-                src_ref=source.at[row, flat],
-                dst_ref=target.at[row, me],
+                src_ref=source.at[row, flat, wire],
+                dst_ref=target.at[row, me, wire],
                 send_sem=sent,
                 recv_sem=received,
                 device_id=flat,
@@ -145,8 +149,8 @@
 
     def wait_chunks(source, target, sent, received, row):
         pltpu.make_async_remote_copy(
-            src_ref=source.at[row, pl.ds(0, devices - 1)],
-            dst_ref=target.at[row, pl.ds(0, devices - 1)],
+            src_ref=source.at[row, pl.ds(0, devices - 1), wire],
+            dst_ref=target.at[row, pl.ds(0, devices - 1), wire],
             send_sem=sent,
             recv_sem=received,
             device_id={"band": band, "lon": lane},
@@ -221,7 +225,45 @@
 
         lax.fori_loop(0, GROUP // 2, one, 0, unroll=4)
 
-    leaving[...] = jnp.zeros_like(leaving)
+    def flip(value):
+        return pltpu.roll(value, main, 1)
+
+    def down(value, count):
+        count = count % value.shape[0]
+        return pltpu.roll(value, count, 0) if count else value
+
+    def places_of(value):
+        row = lax.rem(lax.broadcasted_iota(jnp.int32, value.shape, 0), 8)
+        return row, lax.broadcasted_iota(jnp.int32, value.shape, 1)
+
+    def swap_parts(value):
+        row, column = places_of(value)
+        part = column // rest
+        for bit in (1, 2, 4):
+            row_set, part_set = (row // bit) % 2 == 1, (part // bit) % 2 == 1
+            later = pltpu.roll(down(value, -bit), bit * rest, 1)
+            earlier = pltpu.roll(down(value, bit), LANES - bit * rest, 1)
+            value = jnp.where(
+                row_set == part_set, value, jnp.where(row_set, earlier, later)
+            )
+        return value
+
+    fifth = slice(2 * latitudes, 3 * latitudes)
+
+    def rest_of_coefficients():
+        total = jnp.zeros((latitudes, LANES), jnp.float32)
+        column = lax.broadcasted_iota(jnp.int32, (latitudes, LANES), 1)
+        blank = jnp.zeros((latitudes, LANES - slot_count), jnp.float32)
+        for k in range(entry):
+            held = coefficients[k % own_fields, k // own_fields].astype(jnp.float32)
+            held = jnp.concatenate([held, blank], axis=1)
+            held = pltpu.roll(held, (k * rest - main) % LANES, 1)
+            inside = (column // rest == k) & (column % rest < slot_count - main)
+            total = jnp.where(inside, held, total)
+        return total.astype(jnp.bfloat16)
+
+    if not packed:
+        leaving[...] = jnp.zeros_like(leaving)
     inputs[0].wait()
 
     def gather(group, carry):
@@ -238,8 +280,19 @@
             picked = picked.reshape(GROUP, entry, slot_count).astype(jnp.bfloat16)
             leaving[0, pl.ds(group * GROUP, GROUP), :, 0:slot_count] = picked
         else:
-            picked = picked.reshape(rows, devices, entry, slot_count).astype(jnp.bfloat16)
-            leaving[:, :, :, 0:slot_count] = picked
+            if packed:
+                tail = jnp.dot(
+                    pick[:, fifth], rest_of_coefficients(), preferred_element_type=jnp.float32
+                )
+                blank = jnp.zeros((GROUP * entry, LANES - slot_count), jnp.float32)
+                picked = jnp.concatenate([picked, blank], axis=1)
+                row, column = places_of(picked)
+                first = jnp.where(column < main, picked, flip(down(picked, -4)))
+                picked = jnp.where(row < 4, first, jnp.where(row == 4, tail, 0.0))
+                leaving[...] = picked.reshape(leaving.shape).astype(jnp.bfloat16)
+            else:
+                picked = picked.reshape(rows, devices, entry, slot_count).astype(jnp.bfloat16)
+                leaving[:, :, :, 0:slot_count] = picked
         return carry
 
     if groups > 1:
@@ -259,7 +312,15 @@
         jnp.where(owner, 1.0, 0.0).astype(jnp.bfloat16), earlier, preferred_element_type=jnp.float32
     )
     place = jnp.sum(jnp.where(owner, counts, 0.0), axis=0, keepdims=True)
-    slot_of_pair = pair_band * slot_count + place.astype(jnp.int32)
+    place = place.astype(jnp.int32)
+    if packed:
+        slot_of_pair = jnp.where(
+            place < main,
+            pair_band * main + place,
+            bands * main + pair_band * rest + (place - main),
+        )
+    else:
+        slot_of_pair = pair_band * slot_count + place
     slot = lax.broadcasted_iota(jnp.int32, (padded, half), 0)
     hot = jnp.where(slot == slot_of_pair, 1.0, 0.0).astype(jnp.bfloat16)
     number = lax.broadcasted_iota(jnp.int32, (half, 2 * LANES), 0) + 1
@@ -363,9 +424,29 @@
         pieces = []
         for b in range(bands):
             piece = arrived[i, b * lanes : (b + 1) * lanes].astype(jnp.float32)
-            pieces.append(piece.reshape(stacked, LANES).astype(jnp.bfloat16))
+            pieces.append(piece.reshape(stacked, LANES))
+        if packed:
+            held = pieces
+            row, column = places_of(held[0])
+            columns = []
+            for b in range(0, bands, 2):
+                even, odd = held[b], held[b + 1]
+                left = jnp.where(row < 4, even, flip(down(even, 4)))
+                right = jnp.where(row < 4, flip(odd), down(odd, 4))
+                columns.append(jnp.where(column < main, left, right))
+            tail = jnp.zeros_like(held[0])
+            for b in range(bands):
+                tail = jnp.where(row == b, down(held[b], b - 4), tail)
+            columns.append(swap_parts(tail))
+            return jnp.dot(
+                order_ref[...],
+                jnp.concatenate(columns, axis=1).astype(jnp.bfloat16),
+                preferred_element_type=jnp.float32,
+            )
         by_part = jnp.dot(
-            order_ref[...], jnp.concatenate(pieces, axis=1), preferred_element_type=jnp.float32
+            order_ref[...],
+            jnp.concatenate(pieces, axis=1).astype(jnp.bfloat16),
+            preferred_element_type=jnp.float32,
         )
         columns = [jnp.zeros((stacked, LANES), jnp.float32)] * (padded // LANES)
         for b in range(bands):
@@ -412,9 +493,6 @@
             if h < chunks // 2 - 1:
                 real, imag = real * cosine - imag * sine, real * sine + imag * cosine
 
-    for i in range(rows):
-        row, n, length, inverse = length_of(i)
-        norm = lax.rsqrt(length)
         found = jnp.dot(lhs[i], table[i], preferred_element_type=jnp.float32)
         for h in range(0, chunks, 2):
             pair = []
@@ -428,11 +506,30 @@
             product_ref[i, h * fields : (h + 2) * fields, :] = jnp.concatenate(
                 pair, axis=0
             ).astype(jnp.bfloat16)
-        for j in range(1, lanes):
-            grid_copy(i, j).start()
-        blocks[lane, i] = grid_ref[i, :, block_of(lane)]
+    def finish_packed(i):
+        members = [finished[i, :, m * padded : (m + 1) * padded] for m in range(2)]
+        by_lane = lax.dot_general(
+            order_ref[...],
+            jnp.concatenate(members, axis=0).astype(jnp.bfloat16),
+            (((0,), (0,)), ((), ())),
+            preferred_element_type=jnp.float32,
+        )
+        tail = swap_parts(by_lane[:, bands * main : bands * main + LANES])
+        row, column = places_of(tail)
+        for b in range(bands):
+            held = by_lane[:, b // 2 * LANES : (b // 2 + 1) * LANES]
+            if b % 2 == 0:
+                piece = jnp.where(column < main, held, flip(down(held, -4)))
+            else:
+                piece = jnp.where(column < main, flip(held), down(held, -4))
+            piece = jnp.where(row < 4, piece, down(tail, 4 - b))
+            piece = piece.reshape(lanes, entry, LANES)
+            result[i, b * lanes : (b + 1) * lanes] = piece.astype(jnp.bfloat16)
+        send_chunks(result, returned, back_send_sem.at[i], back_recv_sem.at[i], i, True)
 
     def finish_row(i):
+        if packed:
+            return finish_packed(i)
         spread = []
         for b in range(bands):
             first = b * slot_count
@@ -491,7 +588,17 @@
 
     for i in range(rows):
         for j in range(1, lanes):
+            grid_copy(i, j).start()
+        blocks[lane, i] = grid_ref[i, :, block_of(lane)]
+
+    for i in range(rows):
+        for j in range(1, lanes):
             grid_copy(i, j).wait()
+    if grid_out.ndim == 3:
+        held = blocks[...].astype(jnp.float32).reshape(lanes * rows, fields, points)
+        grid_out[...] = jnp.swapaxes(held, 0, 1).astype(jnp.bfloat16)
+    else:
+        grid_out[...] = blocks[...]
     for i in range(rows):
         wait_chunks(result, returned, back_send_sem.at[i], back_recv_sem.at[i], i)
 
@@ -500,7 +607,28 @@
             held = returned[0, pl.ds(group * GROUP, GROUP)].astype(jnp.float32)
         else:
             held = returned[...].astype(jnp.float32)
-        held = held.reshape(GROUP * entry, LANES).astype(jnp.bfloat16)
+        held = held.reshape(GROUP * entry, LANES)
+        if packed:
+            row, column = places_of(held)
+            held = jnp.where(row < 5, held, 0.0)
+            spread = jnp.where(row < 4, held, flip(down(held, 4)))
+            across = (((0,), (0,)), ((), ()))
+            first = lax.dot_general(
+                pick[...], spread.astype(jnp.bfloat16), across, preferred_element_type=jnp.float32
+            )
+            tail = lax.dot_general(
+                pick[:, fifth],
+                held.astype(jnp.bfloat16),
+                across,
+                preferred_element_type=jnp.float32,
+            )
+            tails = [None] * entry
+            for k in range(entry):
+                at = (k % own_fields) * parts + k // own_fields
+                tails[at] = pltpu.roll(tail, (main - k * rest) % LANES, 1)
+            row, column = places_of(first)
+            return jnp.where(column < main, first, jnp.concatenate(tails, axis=0))
+        held = held.astype(jnp.bfloat16)
         return lax.dot_general(
             pick[...], held, (((0,), (0,)), ((), ())), preferred_element_type=jnp.float32
         )
@@ -529,6 +657,9 @@
     width = 2 * padded
     chunks = lanes * points // CHUNK
     exchange = (rows, devices, entry, LANES)
+    grid_shape = (lanes, rows, fields, points)
+    if lanes * rows == band_rows and band_rows % 8 == 0 and fields % 8 == 0:
+        grid_shape = (fields, band_rows, points)
     bf16, f32 = jnp.bfloat16, jnp.float32
     hbm = pl.BlockSpec(memory_space=pltpu.MemorySpace.HBM)
     return pl.pallas_call(
@@ -536,6 +667,7 @@
         in_specs=[hbm] * 6,
         out_specs=[pl.BlockSpec(memory_space=pltpu.VMEM)] * 2,
         scratch_shapes=[
+            pltpu.VMEM((lanes, rows, fields, points), bf16),
             pltpu.VMEM(coefficients.shape, bf16),
             pltpu.SMEM(cycle_length.shape, jnp.int32),
             pltpu.SMEM(row_latitude.shape, jnp.int32),
@@ -564,7 +696,7 @@
         + [pltpu.SemaphoreType.DMA((lanes,))] * 2
         + [pltpu.SemaphoreType.DMA((rows, lanes))] * 2,
         out_shape=[
-            jax.ShapeDtypeStruct((lanes, rows, fields, points), bf16),
+            jax.ShapeDtypeStruct(grid_shape, bf16),
             jax.ShapeDtypeStruct(coefficients.shape, bf16),
         ],
         compiler_params=pltpu.CompilerParams(
@@ -578,32 +710,27 @@
     )
 
 
-def place_kernel(blocks, placed, grid_out, tendencies_out, grid_ref, sem):
-    tendencies_copy = pltpu.make_async_copy(placed, tendencies_out, sem.at[0])
-    tendencies_copy.start()
-    lanes, rows, fields, points = blocks.shape
-    held = blocks[...].astype(jnp.float32).reshape(lanes * rows, fields, points)
-    grid_ref[...] = jnp.swapaxes(held, 0, 1).astype(jnp.bfloat16)
-    grid_copy = pltpu.make_async_copy(grid_ref, grid_out, sem.at[1])
-    grid_copy.start()
-    tendencies_copy.wait()
-    grid_copy.wait()
-
-
-def place_outputs(blocks, placed):
-    lanes, rows, fields, points = blocks.shape
-    grid_shape = (fields, lanes * rows, points)
+def write_kernel(*refs):
+    count = (len(refs) - 1) // 2
+    copies = [
+        pltpu.make_async_copy(refs[index], refs[count + index], refs[-1].at[index])
+        for index in range(count)
+    ]
+    for copy in copies:
+        copy.start()
+    for copy in copies:
+        copy.wait()
+
+
+def write_outputs(*arrays):
     return pl.pallas_call(
-        place_kernel,
-        in_specs=[pl.BlockSpec(memory_space=pltpu.VMEM)] * 2,
-        out_specs=[pl.BlockSpec(memory_space=pl.ANY)] * 2,
-        out_shape=[
-            jax.ShapeDtypeStruct(grid_shape, jnp.bfloat16),
-            jax.ShapeDtypeStruct(placed.shape, jnp.bfloat16),
-        ],
-        scratch_shapes=[pltpu.VMEM(grid_shape, jnp.bfloat16), pltpu.SemaphoreType.DMA((2,))],
+        write_kernel,
+        in_specs=[pl.BlockSpec(memory_space=pltpu.VMEM)] * len(arrays),
+        out_specs=[pl.BlockSpec(memory_space=pl.ANY)] * len(arrays),
+        out_shape=[jax.ShapeDtypeStruct(array.shape, array.dtype) for array in arrays],
+        scratch_shapes=[pltpu.SemaphoreType.DMA((len(arrays),))],
         compiler_params=pltpu.CompilerParams(vmem_limit_bytes=16 << 20),
-    )(blocks, placed)
+    )(*arrays)
 
 
 def on_device(coefficients, cycle_length, row_latitude, pair_band, gridpoint_factor):
@@ -616,7 +743,7 @@
     places = np.arange(stacked).reshape(lanes, parts, own_fields)
     places = places.transpose(1, 0, 2).reshape(-1)
     order = jnp.asarray(places[:, None] == np.arange(stacked)[None, :], dtype=jnp.bfloat16)
-    blocks, placed = round_trip(
+    grid, placed = round_trip(
         jnp.transpose(coefficients, (0, 2, 3, 1)),
         cycle_length,
         row_latitude,
@@ -626,11 +753,12 @@
         bands,
         lanes,
     )
-    if lanes * own_rows == band_rows and band_rows % 8 == 0 and fields % 8 == 0:
-        grid, placed = place_outputs(blocks, placed)
-        return (grid, jnp.transpose(placed, (0, 3, 1, 2)))
-    grid_rows = blocks.reshape(lanes * own_rows, fields, points)[:band_rows]
-    return (jnp.transpose(grid_rows, (1, 0, 2)), jnp.transpose(placed, (0, 3, 1, 2)))
+    if grid.ndim == 3:
+        grid, placed = write_outputs(grid, placed)
+    else:
+        grid = grid.reshape(lanes * own_rows, fields, points)[:band_rows]
+        grid = jnp.transpose(grid, (1, 0, 2))
+    return (grid, jnp.transpose(placed, (0, 3, 1, 2)))
 
 
 def solution(mesh):

time: 22.8 us -> 22.3 us (0.978)
  Pallas kernels: 22 us -> 21.5 us
    pallas_call x1, Pallas kernels: 21.2 us -> 20.8 us  [round_trip(): pl.pallas_call(functools.partial(round_kernel, bands, lanes), in_specs=[h...]
where the time goes in v3:
time: 22.3 us; the launch traced here: 22.2 us
  Pallas kernels  21.5 us (96%)
  between operations  0.64 us (3%)
    pallas_call x1, Pallas kernels, round_trip(): pl.pallas_call(functools.partial(round_kernel, bands, lanes), in_specs=[h...  20.8 us
    pallas_call x1, Pallas kernels, write_outputs(): pl.pallas_call(write_kernel, in_specs=[pl.BlockSpec(memory_space=pltpu.VM...  0.73 us

profile of v3, /device:TPU:0, one launch (start us, length us, event | category | flops | bytes accessed | tf_op | source)
XLA Modules:
  0.0 22.2 jit_solution(3418059583260203323)
XLA Ops:
  0.6 20.8 %shard_map.77 = (bf16[8,8,1408]{2,1,0:T(8,128)(2,1)S(1)}, bf16[2,4,64,80]{3,2,1,0:T(8,128)(2,1)S(1)}) custom-call(bf16[2,4,64,80]{3,2,1,0:T(8,128)(2,1)} %bitcast.2, s32[64]{0:T(128)} %cycle_hbm.1, s32[64]{0:T(128)} %latitude_hbm.1, s32[640]{0:T(1024)} %pair_band_hbm.1, bf16[8,1408]{1,0:T(8,128)(2,1)} %factor_hbm.1, bf16[32,32]{1,0:T(8,128)(2,1)} %constant.2.clone.order_hbm), custom_call_target="tpu_custom_call" | custom-call | tf_op jit(solution)/shard_map/pallas_call | solution.py:665
  21.4 0.7 %shard_map.78 = (bf16[8,8,1408]{2,1,0:T(8,128)(2,1)}, bf16[2,4,64,80]{3,2,1,0:T(8,128)(2,1)}) custom-call(bf16[8,8,1408]{2,1,0:T(8,128)(2,1)S(1)} %get-tuple-element.6.refs_0_, bf16[2,4,64,80]{3,2,1,0:T(8,128)(2,1)S(1)} %get-tuple-element.7.refs_1_), custom_call_target="tpu_custom_call" | custom-call | tf_op jit(solution)/shard_map/pallas_call | solution.py:726

commit v4 on v3

--- a/solution.py
+++ b/solution.py
@@ -525,7 +525,6 @@
             piece = jnp.where(row < 4, piece, down(tail, 4 - b))
             piece = piece.reshape(lanes, entry, LANES)
             result[i, b * lanes : (b + 1) * lanes] = piece.astype(jnp.bfloat16)
-        send_chunks(result, returned, back_send_sem.at[i], back_recv_sem.at[i], i, True)
 
     def finish_row(i):
         if packed:
@@ -555,7 +554,6 @@
         for b in range(bands):
             piece = by_lane[:, b * LANES : (b + 1) * LANES].reshape(lanes, entry, LANES)
             result[i, b * lanes : (b + 1) * lanes] = piece.astype(jnp.bfloat16)
-        send_chunks(result, returned, back_send_sem.at[i], back_recv_sem.at[i], i, True)
 
     for i in range(rows):
         row, n, length, inverse = length_of(i)
@@ -586,6 +584,7 @@
                 finished[i, t * fields : (t + 1) * fields, columns] = value * scale
         finish_row(i)
 
+    send_chunks(result, returned, back_send_sem, back_recv_sem, every, True)
     for i in range(rows):
         for j in range(1, lanes):
             grid_copy(i, j).start()
@@ -599,8 +598,7 @@
         grid_out[...] = jnp.swapaxes(held, 0, 1).astype(jnp.bfloat16)
     else:
         grid_out[...] = blocks[...]
-    for i in range(rows):
-        wait_chunks(result, returned, back_send_sem.at[i], back_recv_sem.at[i], i)
+    wait_chunks(result, returned, back_send_sem, back_recv_sem, every)
 
     def place_group(group):
         if groups > 1:
@@ -691,8 +689,7 @@
             pltpu.VMEM((rows, 2 * fields, width), f32),
         ]
         + [pltpu.SemaphoreType.DMA((6,))]
-        + [pltpu.SemaphoreType.DMA] * 2
-        + [pltpu.SemaphoreType.DMA((rows,))] * 2
+        + [pltpu.SemaphoreType.DMA] * 4
         + [pltpu.SemaphoreType.DMA((lanes,))] * 2
         + [pltpu.SemaphoreType.DMA((rows, lanes))] * 2,
         out_shape=[

time: 22.3 us -> 22 us (0.987)
  Pallas kernels: 21.5 us -> 21.2 us
    pallas_call x1, Pallas kernels: 20.8 us -> 20.5 us  [round_trip(): pl.pallas_call(functools.partial(round_kernel, bands, lanes), in_specs=[h...]
where the time goes in v4:
time: 22 us; the launch traced here: 21.8 us
  Pallas kernels  21.2 us (96%)
  between operations  0.64 us (3%)
    pallas_call x1, Pallas kernels, round_trip(): pl.pallas_call(functools.partial(round_kernel, bands, lanes), in_specs=[h...  20.5 us
    pallas_call x1, Pallas kernels, write_outputs(): pl.pallas_call(write_kernel, in_specs=[pl.BlockSpec(memory_space=pltpu.VM...  0.73 us

profile of v4, /device:TPU:0, one launch (start us, length us, event | category | flops | bytes accessed | tf_op | source)
XLA Modules:
  0.0 21.8 jit_solution(18318501605063390650)
XLA Ops:
  0.6 20.5 %shard_map.77 = (bf16[8,8,1408]{2,1,0:T(8,128)(2,1)S(1)}, bf16[2,4,64,80]{3,2,1,0:T(8,128)(2,1)S(1)}) custom-call(bf16[2,4,64,80]{3,2,1,0:T(8,128)(2,1)} %bitcast.2, s32[64]{0:T(128)} %cycle_hbm.1, s32[64]{0:T(128)} %latitude_hbm.1, s32[640]{0:T(1024)} %pair_band_hbm.1, bf16[8,1408]{1,0:T(8,128)(2,1)} %factor_hbm.1, bf16[32,32]{1,0:T(8,128)(2,1)} %constant.2.clone.order_hbm), custom_call_target="tpu_custom_call" | custom-call | tf_op jit(solution)/shard_map/pallas_call | solution.py:663
  21.1 0.7 %shard_map.78 = (bf16[8,8,1408]{2,1,0:T(8,128)(2,1)}, bf16[2,4,64,80]{3,2,1,0:T(8,128)(2,1)}) custom-call(bf16[8,8,1408]{2,1,0:T(8,128)(2,1)S(1)} %get-tuple-element.6.refs_0_, bf16[2,4,64,80]{3,2,1,0:T(8,128)(2,1)S(1)} %get-tuple-element.7.refs_1_), custom_call_target="tpu_custom_call" | custom-call | tf_op jit(solution)/shard_map/pallas_call | solution.py:723
